TPU v7x, 512 devices: a whole 4x8x8 slice. The times are simulated.
512 devices in a mesh: ctx: 64 (over x, y, core), head: 8 (over z).
Axes of the slice: x: 4, y: 8, z: 8, core: 2. Of those that a mesh axis runs over, the one named last changes fastest.
Arguments:
- queries: bfloat16 [512, 8192], P('ctx', 'head'), may hold values from -128 to 128
- fresh_span_keys: bfloat16 [512, 1024], P('ctx', 'head'), may hold values from -10 to 10
- fresh_span_values: bfloat16 [512, 1024], P('ctx', 'head'), may hold values from -6 to 6
- context_keys: bfloat16 [262144, 1024], P('ctx', 'head'), may hold values from -6 to 6
- context_values: bfloat16 [262144, 1024], P('ctx', 'head'), may hold values from -12 to 12
- selected: int32 [4, 12], replicated, may hold values from 0 to 63, as said below
- out_weight: bfloat16 [8192, 8192], P('head', 'ctx'), may hold values from -0.0625 to 0.0625
Outputs:
- attended: bfloat16 [512, 8192], P('head', 'ctx')
Inputs may be any that keep to these rules, and one draw needn't show every extreme that they name: `selected`: each row lists 12 different cache blocks, and every row lists the newest block, 63.
All inputs are finite; a program needn't handle non-finite values.
Results may differ from a plain program's by a relative error of at most 0.01345.
Values may be sent and summed in bfloat16 or wider, within the bound.
A program may use at most 64 MiB of HBM per device.

v0:
```python
import math

import jax
import jax.numpy as jnp
from jax import lax
from jax.experimental import pallas as pl
from jax.experimental.pallas import tpu as pltpu
from jax.sharding import PartitionSpec as P

HEAD_SIZE = 128
BLOCK_TOKENS = 4096
QUERY_BLOCK = 128
QUERY_BLOCKS = 4
PICKED = 12
SPAN = 512
NX, NY, NZ = 4, 8, 8
CORE_HEADS = 4
HALF = CORE_HEADS * HEAD_SIZE
WIDE = HALF + HEAD_SIZE
CHIP_TOKENS = 16
ROWS = CORE_HEADS * QUERY_BLOCK
KEY_PIECE = 1024
PIECES = BLOCK_TOKENS // KEY_PIECE
TILES = KEY_PIECE // HEAD_SIZE

EXP2_SCALE = math.log2(math.e) / math.sqrt(HEAD_SIZE)
NEG = -(2.0**100)
NEAR_FIRST = (1, 7, 2, 6, 3, 5, 4)
MESH = pl.DeviceIdType.MESH


def place():
    me = lax.axis_index("ctx")
    core = lax.rem(me, 2)
    chip = me // 2
    return me, chip // NY, lax.rem(chip, NY), core, lax.axis_index("head")


def greet(ids):
    barrier = pltpu.get_barrier_semaphore()
    for device in ids:
        pl.semaphore_signal(barrier, inc=1, device_id=device, device_id_type=MESH)
    pl.semaphore_wait(barrier, len(ids))


def remote(src, dst, send, recv, device):
    return pltpu.make_async_remote_copy(
        src_ref=src,
        dst_ref=dst,
        send_sem=send,
        recv_sem=recv,
        device_id=device,
        device_id_type=MESH,
    )


def gather_kernel(
    q_ref,
    fk_ref,
    fv_ref,
    ck_ref,
    cv_ref,
    qall_ref,
    sk_ref,
    sv_ref,
    pk_ref,
    pv_ref,
    own_sem,
    pair_send,
    pair_recv,
    y_send,
    y_recv,
    x_send,
    x_recv,
):
    me, x, y, core, z = place()
    chip = me // 2
    other = me + 1 - 2 * core

    def device(dx, dy, to=core):
        return ((lax.rem(x + dx, NX) * NY + lax.rem(y + dy, NY)) * 2 + to, z)

    def share(dx, dy):
        return lax.rem(x + NX - dx, NX) * NY + lax.rem(y + NY - dy, NY)

    def chunk(dx, dy):
        return qall_ref.at[pl.ds(share(dx, dy) * 2, 2)]

    greet(
        [(other, z)]
        + [device(0, dy) for dy in range(1, NY)]
        + [device(0, dy, 1 - core) for dy in range(1, NY)]
        + [device(dx, 0) for dx in range(1, NX)]
    )

    own_half = q_ref.at[:, pl.ds(pl.multiple_of(core * HALF, HALF), HALF)]
    other_half = q_ref.at[:, pl.ds(pl.multiple_of((1 - core) * HALF, HALF), HALF)]
    pairs = [
        remote(src, dst, pair_send.at[n], pair_recv.at[n], (other, z))
        for n, (src, dst) in enumerate(
            (
                (other_half, qall_ref.at[me]),
                (fk_ref, sk_ref.at[core]),
                (fv_ref, sv_ref.at[core]),
                (ck_ref, pk_ref),
                (cv_ref, pv_ref),
            )
        )
    ]
    owns = [
        pltpu.make_async_copy(src, dst, own_sem.at[n])
        for n, (src, dst) in enumerate(
            (
                (own_half, qall_ref.at[me]),
                (fk_ref, sk_ref.at[core]),
                (fv_ref, sv_ref.at[core]),
            )
        )
    ]
    pairs[0].start()
    for copy in owns:
        copy.start()
    sends = []
    for dy in (4, 3, 5, 2, 6, 1, 7):
        for side, (src, to) in enumerate(((own_half, core), (other_half, 1 - core))):
            copy = remote(
                src, qall_ref.at[me], y_send.at[side, dy], y_recv.at[side, dy], device(0, dy, to)
            )
            copy.start()
            sends.append(copy)
    for copy in pairs[1:]:
        copy.start()
    owns[0].wait()
    remote(
        other_half, qall_ref.at[other], pair_send.at[0], pair_recv.at[0], (other, z)
    ).wait_recv()

    def along_x(dx, dy):
        copy = remote(
            chunk(0, dy), chunk(0, dy), x_send.at[dx, dy], x_recv.at[dx, dy], device(dx, 0)
        )
        copy.start()
        sends.append(copy)

    for dx in (2, 1, 3):
        along_x(dx, 0)
    for dy in NEAR_FIRST:
        for side, at in enumerate((core, 1 - core)):
            slab = qall_ref.at[share(0, dy) * 2 + at]
            remote(
                own_half, slab, y_send.at[side, dy], y_recv.at[side, dy], device(0, dy)
            ).wait_recv()
        for dx in (2, 1, 3):
            along_x(dx, dy)
    for dy in (0,) + NEAR_FIRST:
        for dx in (1, 3, 2):
            remote(
                chunk(dx, dy), chunk(dx, dy), x_send.at[dx, dy], x_recv.at[dx, dy], device(dx, 0)
            ).wait_recv()
    for copy in sends:
        copy.wait_send()
    for copy in owns[1:]:
        copy.wait()
    pairs[0].wait_send()
    spots = (sk_ref.at[1 - core], sv_ref.at[1 - core], pk_ref, pv_ref)
    for n, copy in enumerate(pairs[1:]):
        copy.wait_send()
        remote(
            spots[n], spots[n], pair_send.at[n + 1], pair_recv.at[n + 1], (other, z)
        ).wait_recv()


def gather(queries, fresh_keys, fresh_values, cache_keys, cache_values):
    anywhere = pl.BlockSpec(memory_space=pl.ANY)
    bf16 = jnp.bfloat16
    dma = pltpu.SemaphoreType.DMA
    return pl.pallas_call(
        gather_kernel,
        out_shape=(
            jax.ShapeDtypeStruct((2 * NX * NY, 8, HALF), bf16),
            jax.ShapeDtypeStruct((2, 8, HEAD_SIZE), bf16),
            jax.ShapeDtypeStruct((2, 8, HEAD_SIZE), bf16),
            jax.ShapeDtypeStruct((BLOCK_TOKENS, HEAD_SIZE), bf16),
            jax.ShapeDtypeStruct((BLOCK_TOKENS, HEAD_SIZE), bf16),
        ),
        in_specs=[anywhere] * 5,
        out_specs=[anywhere] * 5,
        scratch_shapes=[
            dma((3,)),
            dma((5,)),
            dma((5,)),
            dma((2, NY)),
            dma((2, NY)),
            dma((NX, NY)),
            dma((NX, NY)),
        ],
        compiler_params=pltpu.CompilerParams(collective_id=0, has_side_effects=True),
        name="gather_spans",
    )(queries, fresh_keys, fresh_values, cache_keys, cache_values)


def attend_kernel(
    sel_ref,
    q_ref,
    sk_ref,
    sv_ref,
    ck_ref,
    cv_ref,
    pk_ref,
    pv_ref,
    out_ref,
    kbuf,
    vbuf,
    qs,
    m_s,
    l_s,
    acc_s,
    s_buf,
    top_buf,
    sems,
):
    me, x, y, core, z = place()
    chip = me // 2
    copies = [
        pltpu.make_async_copy(src, dst, sems.at[n])
        for n, (src, dst) in enumerate(
            (
                (ck_ref, kbuf.at[0]),
                (cv_ref, vbuf.at[0, :, pl.ds(0, HEAD_SIZE)]),
                (pk_ref, kbuf.at[1]),
                (pv_ref, vbuf.at[1, :, pl.ds(0, HEAD_SIZE)]),
            )
        )
    ]
    for copy in copies:
        copy.start()

    vbuf[:, :, HEAD_SIZE:] = jnp.ones((2, BLOCK_TOKENS, HEAD_SIZE), jnp.bfloat16)
    stat_lane = lax.broadcasted_iota(jnp.int32, (QUERY_BLOCK, HEAD_SIZE), 1)

    @pl.loop(0, QUERY_BLOCKS)
    def _(j):
        start = pl.multiple_of(j * QUERY_BLOCK, QUERY_BLOCK)
        for g in range(CORE_HEADS):
            qs[g * QUERY_BLOCK : (g + 1) * QUERY_BLOCK] = q_ref[
                pl.ds(start, QUERY_BLOCK), g * HEAD_SIZE : (g + 1) * HEAD_SIZE
            ]
        m_s[...] = jnp.full_like(m_s, NEG)
        l_s[...] = jnp.zeros_like(l_s)
        acc_s[...] = jnp.zeros_like(acc_s)

        @pl.when(j >= x)
        def _():
            s = lax.dot_general(
                qs[...], sk_ref[...], (((1,), (1,)), ((), ())), preferred_element_type=jnp.float32
            )
            token = j * QUERY_BLOCK + lax.rem(
                lax.broadcasted_iota(jnp.int32, s.shape, 0), QUERY_BLOCK
            )
            key = chip * CHIP_TOKENS + lax.broadcasted_iota(jnp.int32, s.shape, 1)
            keep = key <= token
            s = jnp.where(keep, s, NEG)
            m = jnp.max(s, axis=1, keepdims=True)
            p = jnp.where(keep, jnp.exp2((s - m) * EXP2_SCALE), 0.0)
            m_s[...] = jnp.broadcast_to(m, m_s.shape)
            l_s[...] = jnp.broadcast_to(jnp.sum(p, axis=1, keepdims=True), l_s.shape)
            acc_s[...] = jnp.dot(
                p.astype(jnp.bfloat16), sv_ref[...], preferred_element_type=jnp.float32
            )

        @pl.when(j == 0)
        def _():
            for copy in copies:
                copy.wait()

        @pl.loop(0, 2)
        def _(b):
            block = jnp.where(b == 0, me, me + 1 - 2 * core)
            wanted = sel_ref[j, 0] == block
            for n in range(1, PICKED):
                wanted = jnp.logical_or(wanted, sel_ref[j, n] == block)

            def score(n):
                keys = kbuf[b, n * KEY_PIECE : (n + 1) * KEY_PIECE, :]
                scores = lax.dot_general(
                    qs[...], keys, (((1,), (1,)), ((), ())), preferred_element_type=jnp.float32
                )
                s_buf[n % 2] = scores
                top = scores[:, :HEAD_SIZE]
                for t in range(1, TILES):
                    top = jnp.maximum(top, scores[:, t * HEAD_SIZE : (t + 1) * HEAD_SIZE])
                top_buf[n % 2] = top

            def weigh(n):
                m_old = m_s[...]
                m_new = jnp.maximum(m_old, jnp.max(top_buf[n % 2], axis=1, keepdims=True))
                shrink = jnp.exp2((m_old - m_new) * EXP2_SCALE)
                m_s[...] = m_new
                parts = []
                for t in range(TILES):
                    part = jnp.exp2(
                        (s_buf[n % 2, :, t * HEAD_SIZE : (t + 1) * HEAD_SIZE] - m_new) * EXP2_SCALE
                    )
                    parts.append(part.astype(jnp.bfloat16))
                both = jnp.dot(
                    jnp.concatenate(parts, axis=1),
                    vbuf[b, n * KEY_PIECE : (n + 1) * KEY_PIECE, :],
                    preferred_element_type=jnp.float32,
                )
                acc_s[...] = acc_s[...] * shrink + both[:, :HEAD_SIZE]
                l_s[...] = l_s[...] * shrink + both[:, HEAD_SIZE:]

            @pl.when(wanted)
            def _():
                score(0)
                for n in range(PIECES):
                    if n + 1 < PIECES:
                        score(n + 1)
                    weigh(n)

        m = m_s[...]
        m_sent = m.astype(jnp.bfloat16).astype(jnp.float32)
        grow = jnp.exp2((m - m_sent) * EXP2_SCALE)
        total = l_s[...] * grow
        high = total.astype(jnp.bfloat16).astype(jnp.float32)
        low = total - high
        acc = acc_s[...] * grow
        stats = jnp.zeros((QUERY_BLOCK, HEAD_SIZE), jnp.float32)
        for g in range(CORE_HEADS):
            here = slice(g * QUERY_BLOCK, (g + 1) * QUERY_BLOCK)
            out_ref[j, :, g * HEAD_SIZE : (g + 1) * HEAD_SIZE] = acc[here].astype(jnp.bfloat16)
            stats = jnp.where(stat_lane == g, m_sent[here], stats)
            stats = jnp.where(stat_lane == CORE_HEADS + g, high[here], stats)
            stats = jnp.where(stat_lane == 2 * CORE_HEADS + g, low[here], stats)
        out_ref[j, :, HALF:WIDE] = stats.astype(jnp.bfloat16)


def attend(selected, q_all, span_keys, span_values, own_k, own_v, pair_k, pair_v):
    anywhere = pl.BlockSpec(memory_space=pl.ANY)
    vmem = pl.BlockSpec(memory_space=pltpu.VMEM)
    f32 = jnp.float32
    return pl.pallas_call(
        attend_kernel,
        out_shape=jax.ShapeDtypeStruct((QUERY_BLOCKS, QUERY_BLOCK, WIDE), jnp.bfloat16),
        in_specs=[pl.BlockSpec(memory_space=pltpu.SMEM), vmem, vmem, vmem] + [anywhere] * 4,
        out_specs=vmem,
        scratch_shapes=[
            pltpu.VMEM((2, BLOCK_TOKENS, HEAD_SIZE), jnp.bfloat16),
            pltpu.VMEM((2, BLOCK_TOKENS, 2 * HEAD_SIZE), jnp.bfloat16),
            pltpu.VMEM((ROWS, HEAD_SIZE), jnp.bfloat16),
            pltpu.VMEM((ROWS, HEAD_SIZE), f32),
            pltpu.VMEM((ROWS, HEAD_SIZE), f32),
            pltpu.VMEM((ROWS, HEAD_SIZE), f32),
            pltpu.VMEM((2, ROWS, KEY_PIECE), f32),
            pltpu.VMEM((2, ROWS, HEAD_SIZE), f32),
            pltpu.SemaphoreType.DMA((4,)),
        ],
        name="attend_blocks",
    )(selected, q_all, span_keys, span_values, own_k, own_v, pair_k, pair_v)


def merge(pieces):
    stats = [piece[:, HALF:WIDE].astype(jnp.float32) for piece in pieces]
    joined = []
    for g in range(CORE_HEADS):
        tops = [stat[:, g : g + 1] for stat in stats]
        top = tops[0]
        for one in tops[1:]:
            top = jnp.maximum(top, one)
        total = jnp.zeros_like(top)
        acc = None
        for piece, stat, one in zip(pieces, stats, tops):
            weight = jnp.exp2((one - top) * EXP2_SCALE)
            total = total + weight * (
                stat[:, CORE_HEADS + g : CORE_HEADS + g + 1]
                + stat[:, 2 * CORE_HEADS + g : 2 * CORE_HEADS + g + 1]
            )
            term = weight * piece[:, g * HEAD_SIZE : (g + 1) * HEAD_SIZE].astype(jnp.float32)
            acc = term if acc is None else acc + term
        joined.append((top, total, acc))
    return joined


def combine_kernel(
    part_ref,
    w_ref,
    out_ref,
    own,
    from_x,
    merged,
    from_y,
    rows,
    partial,
    from_z,
    own_sem,
    x_send,
    x_recv,
    y_send,
    y_recv,
    ay_send,
    ay_recv,
    ax_send,
    ax_recv,
    c_send,
    c_recv,
    z_send,
    z_recv,
):
    me, x, y, core, z = place()
    other = me + 1 - 2 * core
    f32 = jnp.float32

    def device(dx, dy):
        return ((lax.rem(x + dx, NX) * NY + lax.rem(y + dy, NY)) * 2 + core, z)

    greet(
        [(other, z)]
        + [device(0, dy) for dy in range(1, NY)]
        + [device(dx, 0) for dx in range(1, NX)]
        + [(me, lax.rem(z + dz, NZ)) for dz in range(1, NZ)]
    )
    sends = []

    def turn(n):
        return 4 + (1 - 2 * lax.rem(n, 2)) * ((n + 1) // 2)

    def piece(dy):
        at = lax.rem(y + dy, NY)
        return at, pl.ds(pl.multiple_of(at * CHIP_TOKENS, CHIP_TOKENS), CHIP_TOKENS)

    mine = pltpu.make_async_copy(part_ref.at[x], own, own_sem)
    mine.start()

    def to_x(dx, dy):
        _, here = piece(dy)
        return remote(
            part_ref.at[lax.rem(x + dx, NX), here],
            from_x.at[dx, here],
            x_send.at[dx, dy],
            x_recv.at[dx, dy],
            device(dx, 0),
        )

    def to_y(dy):
        return remote(
            merged.at[lax.rem(y + dy, NY)],
            from_y.at[dy],
            y_send.at[dy],
            y_recv.at[dy],
            device(0, dy),
        )

    @pl.loop(0, NY)
    def _(n):
        for dx in (2, 1, 3):
            to_x(dx, turn(n)).start()

    mine.wait()
    stat_lane = lax.broadcasted_iota(jnp.int32, (CHIP_TOKENS, HEAD_SIZE), 1)

    @pl.loop(0, NY)
    def _(n):
        dy = turn(n)
        at, here = piece(dy)
        for dx in range(1, NX):
            spot = from_x.at[dx, here]
            remote(spot, spot, x_send.at[dx, dy], x_recv.at[dx, dy], device(dx, 0)).wait_recv()
        joined = merge([own[here, :]] + [from_x[dx, here, :] for dx in range(1, NX)])
        stats = jnp.zeros((CHIP_TOKENS, HEAD_SIZE), f32)
        for g, (top, total, acc) in enumerate(joined):
            high = total.astype(jnp.bfloat16).astype(f32)
            stats = jnp.where(stat_lane == g, top, stats)
            stats = jnp.where(stat_lane == CORE_HEADS + g, high, stats)
            stats = jnp.where(stat_lane == 2 * CORE_HEADS + g, total - high, stats)
            merged[at, :, g * HEAD_SIZE : (g + 1) * HEAD_SIZE] = acc.astype(jnp.bfloat16)
        merged[at, :, HALF:WIDE] = stats.astype(jnp.bfloat16)

        @pl.when(n > 0)
        def _():
            to_y(turn(n - 1)).start()

    for dy in range(1, NY):
        remote(
            from_y.at[dy], from_y.at[dy], y_send.at[dy], y_recv.at[dy], device(0, dy)
        ).wait_recv()
    joined = merge([merged[y]] + [from_y[dy] for dy in range(1, NY)])
    for g, (_, total, acc) in enumerate(joined):
        rows[x, core, y, :, g * HEAD_SIZE : (g + 1) * HEAD_SIZE] = (acc / total).astype(
            jnp.bfloat16
        )

    def spot(dx, dy):
        return rows.at[lax.rem(x + NX - dx, NX), core, lax.rem(y + NY - dy, NY)]

    for dy in (4, 3, 5, 2, 6, 1, 7):
        copy = remote(spot(0, 0), spot(0, 0), ay_send.at[dy], ay_recv.at[dy], device(0, dy))
        copy.start()
        sends.append(copy)
    for dy in (0,) + NEAR_FIRST:
        if dy:
            remote(
                spot(0, dy), spot(0, dy), ay_send.at[dy], ay_recv.at[dy], device(0, dy)
            ).wait_recv()
        for dx in (2, 1, 3):
            copy = remote(
                spot(0, dy), spot(0, dy), ax_send.at[dx, dy], ax_recv.at[dx, dy], device(dx, 0)
            )
            copy.start()
            sends.append(copy)
    for dx in (0, 1, 3, 2):
        if dx:
            for dy in (0,) + NEAR_FIRST:
                remote(
                    spot(dx, dy), spot(dx, dy), ax_send.at[dx, dy], ax_recv.at[dx, dy], device(dx, 0)
                ).wait_recv()
        group = rows.at[lax.rem(x + NX - dx, NX), core]
        copy = remote(group, group, c_send.at[dx], c_recv.at[dx], (other, z))
        copy.start()
        sends.append(copy)
    for dx in (0, 1, 3, 2):
        at = lax.rem(x + NX - dx, NX)
        group = rows.at[at, 1 - core]
        remote(group, group, c_send.at[dx], c_recv.at[dx], (other, z)).wait_recv()
        product = jnp.dot(
            rows[at, 0].reshape(QUERY_BLOCK, HALF), w_ref[:HALF, :], preferred_element_type=f32
        ) + jnp.dot(
            rows[at, 1].reshape(QUERY_BLOCK, HALF), w_ref[HALF:, :], preferred_element_type=f32
        )
        product = product.astype(jnp.bfloat16)
        for half in range(2):
            to = 2 * at + half
            partial[to] = product[half * 64 : (half + 1) * 64]
        for half in range(2):
            to = 2 * at + half

            @pl.when(to != z)
            def _():
                remote(
                    partial.at[to], from_z.at[z], z_send.at[to], z_recv.at[z], (me, to)
                ).start()

    total = partial[z].astype(f32)
    for dz in range(1, NZ):
        source = lax.rem(z + dz, NZ)
        copy = remote(
            partial.at[source], from_z.at[source], z_send.at[source], z_recv.at[source], (me, source)
        )
        copy.wait_send()
        copy.wait_recv()
        total = total + from_z[source].astype(f32)
    out_ref[...] = total.astype(jnp.bfloat16)

    @pl.loop(0, NY)
    def _(dy):
        for dx in range(1, NX):
            to_x(dx, dy).wait_send()

        @pl.when(dy > 0)
        def _():
            to_y(dy).wait_send()

    for copy in sends:
        copy.wait_send()


def combine(parts, out_weight):
    vmem = pl.BlockSpec(memory_space=pltpu.VMEM)
    bf16 = jnp.bfloat16
    dma = pltpu.SemaphoreType.DMA
    return pl.pallas_call(
        combine_kernel,
        out_shape=jax.ShapeDtypeStruct((SPAN // NZ, HEAD_SIZE), bf16),
        in_specs=[pl.BlockSpec(memory_space=pl.ANY), vmem],
        out_specs=vmem,
        scratch_shapes=[
            pltpu.VMEM((QUERY_BLOCK, WIDE), bf16),
            pltpu.VMEM((NX, QUERY_BLOCK, WIDE), bf16),
            pltpu.VMEM((NY, CHIP_TOKENS, WIDE), bf16),
            pltpu.VMEM((NY, CHIP_TOKENS, WIDE), bf16),
            pltpu.VMEM((NX, 2, NY, CHIP_TOKENS, HALF), bf16),
            pltpu.VMEM((NZ, SPAN // NZ, HEAD_SIZE), bf16),
            pltpu.VMEM((NZ, SPAN // NZ, HEAD_SIZE), bf16),
            dma,
            dma((NX, NY)),
            dma((NX, NY)),
            dma((NY,)),
            dma((NY,)),
            dma((NY,)),
            dma((NY,)),
            dma((NX, NY)),
            dma((NX, NY)),
            dma((NX,)),
            dma((NX,)),
            dma((NZ,)),
            dma((NZ,)),
        ],
        compiler_params=pltpu.CompilerParams(collective_id=1, has_side_effects=True),
        name="combine_rows",
    )(parts, out_weight)


def local(
    queries, fresh_span_keys, fresh_span_values, context_keys, context_values, selected, out_weight
):
    q_all, span_keys, span_values, pair_k, pair_v = gather(
        queries, fresh_span_keys, fresh_span_values, context_keys, context_values
    )
    parts = attend(
        selected,
        q_all.reshape(SPAN, HALF),
        span_keys.reshape(CHIP_TOKENS, HEAD_SIZE),
        span_values.reshape(CHIP_TOKENS, HEAD_SIZE),
        context_keys,
        context_values,
        pair_k,
        pair_v,
    )
    return combine(parts, out_weight)


def solution(mesh):
    return jax.shard_map(
        local,
        mesh=mesh,
        in_specs=(
            P("ctx", "head"),
            P("ctx", "head"),
            P("ctx", "head"),
            P("ctx", "head"),
            P("ctx", "head"),
            P(),
            P("head", "ctx"),
        ),
        out_specs=P("head", "ctx"),
        check_vma=False,
    )
```

profile of v0, /device:TPU:6, one launch (start us, length us, event | category | flops | bytes accessed | tf_op | source)
XLA Modules:
  0.0 79.0 jit_solution(10058794679395441087)
XLA Ops:
  0.0 20.2 %gather_spans.1 = (bf16[64,8,512]{2,1,0:T(8,128)(2,1)}, bf16[2,8,128]{2,1,0:T(8,128)(2,1)}, bf16[2,8,128]{2,1,0:T(8,128)(2,1)}, bf16[4096,128]{1,0:T(8,128)(2,1)}, bf16[4096,128]{1,0:T(8,128)(2,1)}) custom-call(bf16[8,1024]{1,0:T(8,128)(2,1)} %q_ref.1, bf16[8,128]{1,0:T(8,128)(2,1)} %fk_ref.1, bf16[8,128]{1,0:T(8,128)(2,1)} %fv_ref.1, ...), custom_call_target="tpu_custom_call" | custom-call | tf_op jit(solution)/shard_map/gather_spans/pallas_call | solution.py:177
  20.2 13.3 %attend_blocks.1.part_ref = bf16[4,128,640]{2,1,0:T(8,128)(2,1)} custom-call(s32[4,12]{1,0:T(4,128)} %sel_ref.1, bf16[512,512]{1,0:T(8,128)(2,1)} %bitcast.3, bf16[16,128]{1,0:T(8,128)(2,1)} %bitcast.4, bf16[16,128]{1,0:T(8,128)(2,1)} %bitcast.5, bf16[4096,128]{1,0:T(8,128)(2,1)} %ck_ref.3, bf16[4096,128]{1,0:T(8,128)(2,1)} %cv_ref.3, ...), custom_call_target="tpu_custom_call" | custom-call | tf_op jit(solution)/shard_map/attend_blocks/pallas_call | solution.py:342
  33.6 44.1 %combine_rows.1 = bf16[64,128]{1,0:T(8,128)(2,1)} custom-call(bf16[4,128,640]{2,1,0:T(8,128)(2,1)} %attend_blocks.1.part_ref, bf16[1024,128]{1,0:T(8,128)(2,1)} %w_ref.1), custom_call_target="tpu_custom_call" | custom-call | tf_op jit(solution)/shard_map/combine_rows/pallas_call | solution.py:570
  77.6 1.3 %copy.9 = bf16[64,128]{1,0:T(8,128)(2,1)} copy(bf16[64,128]{1,0:T(8,128)(2,1)} %combine_rows.1) | data formatting | bytes 32768
where the time goes:
time: 79.3 us; the launch traced here: 79 us
  Pallas kernels  77.6 us (98%)
  local copies, waits for them, and re-layouts  1.32 us (2%)
    pallas_call x1, Pallas kernels, combine(): pl.pallas_call(combine_kernel, out_shape=jax.ShapeDtypeStruct((SPAN // NZ...  44.1 us
    pallas_call x1, Pallas kernels, gather(): pl.pallas_call(gather_kernel, out_shape=(jax.ShapeDtypeStruct((2 * NX * N...  20.2 us
    pallas_call x1, Pallas kernels, attend(): pl.pallas_call(attend_kernel, out_shape=jax.ShapeDtypeStruct((QUERY_BLOCK...  13.3 us

commit v1 on v0

--- a/solution.py
+++ b/solution.py
@@ -54,7 +54,116 @@
     )
 
 
+def stack_heads(qs, q_ref, start):
+    for g in range(CORE_HEADS):
+        qs[g * QUERY_BLOCK : (g + 1) * QUERY_BLOCK] = q_ref[
+            pl.ds(start, QUERY_BLOCK), g * HEAD_SIZE : (g + 1) * HEAD_SIZE
+        ]
+
+
+def attend_span(chip, j, state, sk_ref, sv_ref):
+    qs, m_s, l_s, acc_s = state
+    s = lax.dot_general(
+        qs[...], sk_ref[...], (((1,), (1,)), ((), ())), preferred_element_type=jnp.float32
+    )
+    token = j * QUERY_BLOCK + lax.rem(lax.broadcasted_iota(jnp.int32, s.shape, 0), QUERY_BLOCK)
+    key = chip * CHIP_TOKENS + lax.broadcasted_iota(jnp.int32, s.shape, 1)
+    keep = key <= token
+    s = jnp.where(keep, s, NEG)
+    m = jnp.max(s, axis=1, keepdims=True)
+    p = jnp.where(keep, jnp.exp2((s - m) * EXP2_SCALE), 0.0)
+    m_s[...] = jnp.broadcast_to(m, m_s.shape)
+    l_s[...] = jnp.broadcast_to(jnp.sum(p, axis=1, keepdims=True), l_s.shape)
+    acc_s[...] = jnp.dot(p.astype(jnp.bfloat16), sv_ref[...], preferred_element_type=jnp.float32)
+
+
+def attend_block(b, state, kbuf, vbuf, s_buf, top_buf, hide=None):
+    qs, m_s, l_s, acc_s = state
+
+    def score(n):
+        keys = kbuf[b, n * KEY_PIECE : (n + 1) * KEY_PIECE, :]
+        scores = lax.dot_general(
+            qs[...], keys, (((1,), (1,)), ((), ())), preferred_element_type=jnp.float32
+        )
+        s_buf[n % 2] = scores
+        top = scores[:, :HEAD_SIZE]
+        for t in range(1, TILES):
+            top = jnp.maximum(top, scores[:, t * HEAD_SIZE : (t + 1) * HEAD_SIZE])
+        top_buf[n % 2] = top
+
+    def weigh(n):
+        m_old = m_s[...]
+        top = jnp.max(top_buf[n % 2], axis=1, keepdims=True)
+        if hide is not None:
+            top = top - hide
+        m_new = jnp.maximum(m_old, top)
+        shrink = jnp.exp2((m_old - m_new) * EXP2_SCALE)
+        m_s[...] = m_new
+        shift = m_new if hide is None else m_new + hide
+        parts = []
+        for t in range(TILES):
+            part = jnp.exp2(
+                (s_buf[n % 2, :, t * HEAD_SIZE : (t + 1) * HEAD_SIZE] - shift) * EXP2_SCALE
+            )
+            parts.append(part.astype(jnp.bfloat16))
+        both = jnp.dot(
+            jnp.concatenate(parts, axis=1),
+            vbuf[b, n * KEY_PIECE : (n + 1) * KEY_PIECE, :],
+            preferred_element_type=jnp.float32,
+        )
+        acc_s[...] = acc_s[...] * shrink + both[:, :HEAD_SIZE]
+        l_s[...] = l_s[...] * shrink + both[:, HEAD_SIZE:]
+
+    score(0)
+    for n in range(PIECES):
+        if n + 1 < PIECES:
+            score(n + 1)
+        weigh(n)
+
+
+def store_partial(out_ref, state):
+    _, m_s, l_s, acc_s = state
+    stat_lane = lax.broadcasted_iota(jnp.int32, (QUERY_BLOCK, HEAD_SIZE), 1)
+    m = m_s[...]
+    m_sent = m.astype(jnp.bfloat16).astype(jnp.float32)
+    grow = jnp.exp2((m - m_sent) * EXP2_SCALE)
+    total = l_s[...] * grow
+    high = total.astype(jnp.bfloat16).astype(jnp.float32)
+    low = total - high
+    acc = acc_s[...] * grow
+    stats = jnp.zeros((QUERY_BLOCK, HEAD_SIZE), jnp.float32)
+    for g in range(CORE_HEADS):
+        here = slice(g * QUERY_BLOCK, (g + 1) * QUERY_BLOCK)
+        out_ref[:, g * HEAD_SIZE : (g + 1) * HEAD_SIZE] = acc[here].astype(jnp.bfloat16)
+        stats = jnp.where(stat_lane == g, m_sent[here], stats)
+        stats = jnp.where(stat_lane == CORE_HEADS + g, high[here], stats)
+        stats = jnp.where(stat_lane == 2 * CORE_HEADS + g, low[here], stats)
+    out_ref[:, HALF:WIDE] = stats.astype(jnp.bfloat16)
+
+
+def is_wanted(sel_ref, j, block):
+    wanted = sel_ref[j, 0] == block
+    for n in range(1, PICKED):
+        wanted = jnp.logical_or(wanted, sel_ref[j, n] == block)
+    return wanted
+
+
+def attention_scratch():
+    f32 = jnp.float32
+    return [
+        pltpu.VMEM((2, BLOCK_TOKENS, HEAD_SIZE), jnp.bfloat16),
+        pltpu.VMEM((2, BLOCK_TOKENS, 2 * HEAD_SIZE), jnp.bfloat16),
+        pltpu.VMEM((ROWS, HEAD_SIZE), jnp.bfloat16),
+        pltpu.VMEM((ROWS, HEAD_SIZE), f32),
+        pltpu.VMEM((ROWS, HEAD_SIZE), f32),
+        pltpu.VMEM((ROWS, HEAD_SIZE), f32),
+        pltpu.VMEM((2, ROWS, KEY_PIECE), f32),
+        pltpu.VMEM((2, ROWS, HEAD_SIZE), f32),
+    ]
+
+
 def gather_kernel(
+    sel_ref,
     q_ref,
     fk_ref,
     fv_ref,
@@ -65,6 +174,20 @@
     sv_ref,
     pk_ref,
     pv_ref,
+    part_ref,
+    kbuf,
+    vbuf,
+    qs,
+    m_s,
+    l_s,
+    acc_s,
+    s_buf,
+    top_buf,
+    q_own,
+    sk_own,
+    sv_own,
+    part_own,
+    load_sem,
     own_sem,
     pair_send,
     pair_recv,
@@ -80,11 +203,18 @@
     def device(dx, dy, to=core):
         return ((lax.rem(x + dx, NX) * NY + lax.rem(y + dy, NY)) * 2 + to, z)
 
+    def own_span(ref, at):
+        return ref.at[pl.ds(pl.multiple_of(at * 8, 8), 8)]
+
     def share(dx, dy):
         return lax.rem(x + NX - dx, NX) * NY + lax.rem(y + NY - dy, NY)
 
     def chunk(dx, dy):
-        return qall_ref.at[pl.ds(share(dx, dy) * 2, 2)]
+        at = pl.multiple_of(share(dx, dy) * CHIP_TOKENS, CHIP_TOKENS)
+        return qall_ref.at[pl.ds(at, CHIP_TOKENS)]
+
+    def slab(device_at):
+        return qall_ref.at[pl.ds(pl.multiple_of(device_at * 8, 8), 8)]
 
     greet(
         [(other, z)]
@@ -99,9 +229,9 @@
         remote(src, dst, pair_send.at[n], pair_recv.at[n], (other, z))
         for n, (src, dst) in enumerate(
             (
-                (other_half, qall_ref.at[me]),
-                (fk_ref, sk_ref.at[core]),
-                (fv_ref, sv_ref.at[core]),
+                (other_half, slab(me)),
+                (fk_ref, own_span(sk_ref, core)),
+                (fv_ref, own_span(sv_ref, core)),
                 (ck_ref, pk_ref),
                 (cv_ref, pv_ref),
             )
@@ -111,9 +241,9 @@
         pltpu.make_async_copy(src, dst, own_sem.at[n])
         for n, (src, dst) in enumerate(
             (
-                (own_half, qall_ref.at[me]),
-                (fk_ref, sk_ref.at[core]),
-                (fv_ref, sv_ref.at[core]),
+                (own_half, slab(me)),
+                (fk_ref, own_span(sk_ref, core)),
+                (fv_ref, own_span(sv_ref, core)),
             )
         )
     ]
@@ -124,15 +254,32 @@
     for dy in (4, 3, 5, 2, 6, 1, 7):
         for side, (src, to) in enumerate(((own_half, core), (other_half, 1 - core))):
             copy = remote(
-                src, qall_ref.at[me], y_send.at[side, dy], y_recv.at[side, dy], device(0, dy, to)
+                src, slab(me), y_send.at[side, dy], y_recv.at[side, dy], device(0, dy, to)
             )
             copy.start()
             sends.append(copy)
     for copy in pairs[1:]:
         copy.start()
+
+    def load(n, src, dst):
+        return pltpu.make_async_copy(src, dst, load_sem.at[n])
+
+    values = pl.ds(0, HEAD_SIZE)
+    loads = [
+        load(0, ck_ref, kbuf.at[0]),
+        load(1, cv_ref, vbuf.at[0, :, values]),
+        load(2, pk_ref, kbuf.at[1]),
+        load(3, pv_ref, vbuf.at[1, :, values]),
+        load(4, qall_ref.at[pl.ds(pl.multiple_of(x * QUERY_BLOCK, QUERY_BLOCK), QUERY_BLOCK)], q_own),
+        load(5, sk_ref, sk_own),
+        load(6, sv_ref, sv_own),
+    ]
+    loads[0].start()
+    loads[1].start()
+    vbuf[:, :, HEAD_SIZE:] = jnp.ones((2, BLOCK_TOKENS, HEAD_SIZE), jnp.bfloat16)
     owns[0].wait()
     remote(
-        other_half, qall_ref.at[other], pair_send.at[0], pair_recv.at[0], (other, z)
+        other_half, slab(other), pair_send.at[0], pair_recv.at[0], (other, z)
     ).wait_recv()
 
     def along_x(dx, dy):
@@ -146,46 +293,72 @@
         along_x(dx, 0)
     for dy in NEAR_FIRST:
         for side, at in enumerate((core, 1 - core)):
-            slab = qall_ref.at[share(0, dy) * 2 + at]
+            spot = slab(share(0, dy) * 2 + at)
             remote(
-                own_half, slab, y_send.at[side, dy], y_recv.at[side, dy], device(0, dy)
+                own_half, spot, y_send.at[side, dy], y_recv.at[side, dy], device(0, dy)
             ).wait_recv()
         for dx in (2, 1, 3):
             along_x(dx, dy)
+    loads[4].start()
+    spots = (own_span(sk_ref, 1 - core), own_span(sv_ref, 1 - core), pk_ref, pv_ref)
+    for n, spot in enumerate(spots):
+        remote(spot, spot, pair_send.at[n + 1], pair_recv.at[n + 1], (other, z)).wait_recv()
+    for copy in owns[1:]:
+        copy.wait()
+    for n in (5, 6, 2, 3):
+        loads[n].start()
+    for n in (4, 5, 6):
+        loads[n].wait()
+
+    state = (qs, m_s, l_s, acc_s)
+    stack_heads(qs, q_own, 0)
+    attend_span(chip, x, state, sk_own, sv_own)
+    for n in range(4):
+        loads[n].wait()
+
+    @pl.loop(0, 2)
+    def _(b):
+        block = jnp.where(b == 0, me, other)
+        hide = jnp.where(is_wanted(sel_ref, x, block), 0.0, -2.0 * NEG)
+        attend_block(b, state, kbuf, vbuf, s_buf, top_buf, hide)
+
+    store_partial(part_own, state)
+    result = load(7, part_own, part_ref)
+    result.start()
+
     for dy in (0,) + NEAR_FIRST:
         for dx in (1, 3, 2):
             remote(
                 chunk(dx, dy), chunk(dx, dy), x_send.at[dx, dy], x_recv.at[dx, dy], device(dx, 0)
             ).wait_recv()
-    for copy in sends:
+    for copy in sends + pairs:
         copy.wait_send()
-    for copy in owns[1:]:
-        copy.wait()
-    pairs[0].wait_send()
-    spots = (sk_ref.at[1 - core], sv_ref.at[1 - core], pk_ref, pv_ref)
-    for n, copy in enumerate(pairs[1:]):
-        copy.wait_send()
-        remote(
-            spots[n], spots[n], pair_send.at[n + 1], pair_recv.at[n + 1], (other, z)
-        ).wait_recv()
-
-
-def gather(queries, fresh_keys, fresh_values, cache_keys, cache_values):
+    result.wait()
+
+
+def gather(selected, queries, fresh_keys, fresh_values, cache_keys, cache_values):
     anywhere = pl.BlockSpec(memory_space=pl.ANY)
     bf16 = jnp.bfloat16
     dma = pltpu.SemaphoreType.DMA
     return pl.pallas_call(
         gather_kernel,
         out_shape=(
-            jax.ShapeDtypeStruct((2 * NX * NY, 8, HALF), bf16),
-            jax.ShapeDtypeStruct((2, 8, HEAD_SIZE), bf16),
-            jax.ShapeDtypeStruct((2, 8, HEAD_SIZE), bf16),
+            jax.ShapeDtypeStruct((SPAN, HALF), bf16),
+            jax.ShapeDtypeStruct((CHIP_TOKENS, HEAD_SIZE), bf16),
+            jax.ShapeDtypeStruct((CHIP_TOKENS, HEAD_SIZE), bf16),
             jax.ShapeDtypeStruct((BLOCK_TOKENS, HEAD_SIZE), bf16),
             jax.ShapeDtypeStruct((BLOCK_TOKENS, HEAD_SIZE), bf16),
+            jax.ShapeDtypeStruct((QUERY_BLOCK, WIDE), bf16),
         ),
-        in_specs=[anywhere] * 5,
-        out_specs=[anywhere] * 5,
-        scratch_shapes=[
+        in_specs=[pl.BlockSpec(memory_space=pltpu.SMEM)] + [anywhere] * 5,
+        out_specs=[anywhere] * 6,
+        scratch_shapes=attention_scratch()
+        + [
+            pltpu.VMEM((QUERY_BLOCK, HALF), bf16),
+            pltpu.VMEM((CHIP_TOKENS, HEAD_SIZE), bf16),
+            pltpu.VMEM((CHIP_TOKENS, HEAD_SIZE), bf16),
+            pltpu.VMEM((QUERY_BLOCK, WIDE), bf16),
+            dma((8,)),
             dma((3,)),
             dma((5,)),
             dma((5,)),
@@ -196,7 +369,7 @@
         ],
         compiler_params=pltpu.CompilerParams(collective_id=0, has_side_effects=True),
         name="gather_spans",
-    )(queries, fresh_keys, fresh_values, cache_keys, cache_values)
+    )(selected, queries, fresh_keys, fresh_values, cache_keys, cache_values)
 
 
 def attend_kernel(
@@ -221,6 +394,7 @@
 ):
     me, x, y, core, z = place()
     chip = me // 2
+    state = (qs, m_s, l_s, acc_s)
     copies = [
         pltpu.make_async_copy(src, dst, sems.at[n])
         for n, (src, dst) in enumerate(
@@ -234,41 +408,21 @@
     ]
     for copy in copies:
         copy.start()
-
     vbuf[:, :, HEAD_SIZE:] = jnp.ones((2, BLOCK_TOKENS, HEAD_SIZE), jnp.bfloat16)
-    stat_lane = lax.broadcasted_iota(jnp.int32, (QUERY_BLOCK, HEAD_SIZE), 1)
-
-    @pl.loop(0, QUERY_BLOCKS)
-    def _(j):
-        start = pl.multiple_of(j * QUERY_BLOCK, QUERY_BLOCK)
-        for g in range(CORE_HEADS):
-            qs[g * QUERY_BLOCK : (g + 1) * QUERY_BLOCK] = q_ref[
-                pl.ds(start, QUERY_BLOCK), g * HEAD_SIZE : (g + 1) * HEAD_SIZE
-            ]
+
+    @pl.loop(1, QUERY_BLOCKS)
+    def _(n):
+        j = lax.rem(x + n, QUERY_BLOCKS)
+        stack_heads(qs, q_ref, pl.multiple_of(j * QUERY_BLOCK, QUERY_BLOCK))
         m_s[...] = jnp.full_like(m_s, NEG)
         l_s[...] = jnp.zeros_like(l_s)
         acc_s[...] = jnp.zeros_like(acc_s)
 
-        @pl.when(j >= x)
+        @pl.when(j > x)
         def _():
-            s = lax.dot_general(
-                qs[...], sk_ref[...], (((1,), (1,)), ((), ())), preferred_element_type=jnp.float32
-            )
-            token = j * QUERY_BLOCK + lax.rem(
-                lax.broadcasted_iota(jnp.int32, s.shape, 0), QUERY_BLOCK
-            )
-            key = chip * CHIP_TOKENS + lax.broadcasted_iota(jnp.int32, s.shape, 1)
-            keep = key <= token
-            s = jnp.where(keep, s, NEG)
-            m = jnp.max(s, axis=1, keepdims=True)
-            p = jnp.where(keep, jnp.exp2((s - m) * EXP2_SCALE), 0.0)
-            m_s[...] = jnp.broadcast_to(m, m_s.shape)
-            l_s[...] = jnp.broadcast_to(jnp.sum(p, axis=1, keepdims=True), l_s.shape)
-            acc_s[...] = jnp.dot(
-                p.astype(jnp.bfloat16), sv_ref[...], preferred_element_type=jnp.float32
-            )
-
-        @pl.when(j == 0)
+            attend_span(chip, j, state, sk_ref, sv_ref)
+
+        @pl.when(n == 1)
         def _():
             for copy in copies:
                 copy.wait()
@@ -276,85 +430,23 @@
         @pl.loop(0, 2)
         def _(b):
             block = jnp.where(b == 0, me, me + 1 - 2 * core)
-            wanted = sel_ref[j, 0] == block
-            for n in range(1, PICKED):
-                wanted = jnp.logical_or(wanted, sel_ref[j, n] == block)
-
-            def score(n):
-                keys = kbuf[b, n * KEY_PIECE : (n + 1) * KEY_PIECE, :]
-                scores = lax.dot_general(
-                    qs[...], keys, (((1,), (1,)), ((), ())), preferred_element_type=jnp.float32
-                )
-                s_buf[n % 2] = scores
-                top = scores[:, :HEAD_SIZE]
-                for t in range(1, TILES):
-                    top = jnp.maximum(top, scores[:, t * HEAD_SIZE : (t + 1) * HEAD_SIZE])
-                top_buf[n % 2] = top
-
-            def weigh(n):
-                m_old = m_s[...]
-                m_new = jnp.maximum(m_old, jnp.max(top_buf[n % 2], axis=1, keepdims=True))
-                shrink = jnp.exp2((m_old - m_new) * EXP2_SCALE)
-                m_s[...] = m_new
-                parts = []
-                for t in range(TILES):
-                    part = jnp.exp2(
-                        (s_buf[n % 2, :, t * HEAD_SIZE : (t + 1) * HEAD_SIZE] - m_new) * EXP2_SCALE
-                    )
-                    parts.append(part.astype(jnp.bfloat16))
-                both = jnp.dot(
-                    jnp.concatenate(parts, axis=1),
-                    vbuf[b, n * KEY_PIECE : (n + 1) * KEY_PIECE, :],
-                    preferred_element_type=jnp.float32,
-                )
-                acc_s[...] = acc_s[...] * shrink + both[:, :HEAD_SIZE]
-                l_s[...] = l_s[...] * shrink + both[:, HEAD_SIZE:]
-
-            @pl.when(wanted)
+
+            @pl.when(is_wanted(sel_ref, j, block))
             def _():
-                score(0)
-                for n in range(PIECES):
-                    if n + 1 < PIECES:
-                        score(n + 1)
-                    weigh(n)
-
-        m = m_s[...]
-        m_sent = m.astype(jnp.bfloat16).astype(jnp.float32)
-        grow = jnp.exp2((m - m_sent) * EXP2_SCALE)
-        total = l_s[...] * grow
-        high = total.astype(jnp.bfloat16).astype(jnp.float32)
-        low = total - high
-        acc = acc_s[...] * grow
-        stats = jnp.zeros((QUERY_BLOCK, HEAD_SIZE), jnp.float32)
-        for g in range(CORE_HEADS):
-            here = slice(g * QUERY_BLOCK, (g + 1) * QUERY_BLOCK)
-            out_ref[j, :, g * HEAD_SIZE : (g + 1) * HEAD_SIZE] = acc[here].astype(jnp.bfloat16)
-            stats = jnp.where(stat_lane == g, m_sent[here], stats)
-            stats = jnp.where(stat_lane == CORE_HEADS + g, high[here], stats)
-            stats = jnp.where(stat_lane == 2 * CORE_HEADS + g, low[here], stats)
-        out_ref[j, :, HALF:WIDE] = stats.astype(jnp.bfloat16)
+                attend_block(b, state, kbuf, vbuf, s_buf, top_buf)
+
+        store_partial(out_ref.at[j], state)
 
 
 def attend(selected, q_all, span_keys, span_values, own_k, own_v, pair_k, pair_v):
     anywhere = pl.BlockSpec(memory_space=pl.ANY)
     vmem = pl.BlockSpec(memory_space=pltpu.VMEM)
-    f32 = jnp.float32
     return pl.pallas_call(
         attend_kernel,
         out_shape=jax.ShapeDtypeStruct((QUERY_BLOCKS, QUERY_BLOCK, WIDE), jnp.bfloat16),
         in_specs=[pl.BlockSpec(memory_space=pltpu.SMEM), vmem, vmem, vmem] + [anywhere] * 4,
         out_specs=vmem,
-        scratch_shapes=[
-            pltpu.VMEM((2, BLOCK_TOKENS, HEAD_SIZE), jnp.bfloat16),
-            pltpu.VMEM((2, BLOCK_TOKENS, 2 * HEAD_SIZE), jnp.bfloat16),
-            pltpu.VMEM((ROWS, HEAD_SIZE), jnp.bfloat16),
-            pltpu.VMEM((ROWS, HEAD_SIZE), f32),
-            pltpu.VMEM((ROWS, HEAD_SIZE), f32),
-            pltpu.VMEM((ROWS, HEAD_SIZE), f32),
-            pltpu.VMEM((2, ROWS, KEY_PIECE), f32),
-            pltpu.VMEM((2, ROWS, HEAD_SIZE), f32),
-            pltpu.SemaphoreType.DMA((4,)),
-        ],
+        scratch_shapes=attention_scratch() + [pltpu.SemaphoreType.DMA((4,))],
         name="attend_blocks",
     )(selected, q_all, span_keys, span_values, own_k, own_v, pair_k, pair_v)
 
@@ -382,6 +474,7 @@
 
 
 def combine_kernel(
+    own_part_ref,
     part_ref,
     w_ref,
     out_ref,
@@ -428,7 +521,7 @@
         at = lax.rem(y + dy, NY)
         return at, pl.ds(pl.multiple_of(at * CHIP_TOKENS, CHIP_TOKENS), CHIP_TOKENS)
 
-    mine = pltpu.make_async_copy(part_ref.at[x], own, own_sem)
+    mine = pltpu.make_async_copy(own_part_ref, own, own_sem)
     mine.start()
 
     def to_x(dx, dy):
@@ -507,17 +600,13 @@
             )
             copy.start()
             sends.append(copy)
-    for dx in (0, 1, 3, 2):
-        if dx:
-            for dy in (0,) + NEAR_FIRST:
-                remote(
-                    spot(dx, dy), spot(dx, dy), ax_send.at[dx, dy], ax_recv.at[dx, dy], device(dx, 0)
-                ).wait_recv()
+    def swap(dx):
         group = rows.at[lax.rem(x + NX - dx, NX), core]
         copy = remote(group, group, c_send.at[dx], c_recv.at[dx], (other, z))
         copy.start()
         sends.append(copy)
-    for dx in (0, 1, 3, 2):
+
+    def project(dx):
         at = lax.rem(x + NX - dx, NX)
         group = rows.at[at, 1 - core]
         remote(group, group, c_send.at[dx], c_recv.at[dx], (other, z)).wait_recv()
@@ -528,8 +617,7 @@
         )
         product = product.astype(jnp.bfloat16)
         for half in range(2):
-            to = 2 * at + half
-            partial[to] = product[half * 64 : (half + 1) * 64]
+            partial[2 * at + half] = product[half * 64 : (half + 1) * 64]
         for half in range(2):
             to = 2 * at + half
 
@@ -539,6 +627,17 @@
                     partial.at[to], from_z.at[z], z_send.at[to], z_recv.at[z], (me, to)
                 ).start()
 
+    swap(0)
+    project(0)
+    for dx in (1, 3, 2):
+        for dy in (0,) + NEAR_FIRST:
+            remote(
+                spot(dx, dy), spot(dx, dy), ax_send.at[dx, dy], ax_recv.at[dx, dy], device(dx, 0)
+            ).wait_recv()
+        swap(dx)
+    for dx in (1, 3, 2):
+        project(dx)
+
     total = partial[z].astype(f32)
     for dz in range(1, NZ):
         source = lax.rem(z + dz, NZ)
@@ -563,14 +662,14 @@
         copy.wait_send()
 
 
-def combine(parts, out_weight):
+def combine(own_part, parts, out_weight):
     vmem = pl.BlockSpec(memory_space=pltpu.VMEM)
     bf16 = jnp.bfloat16
     dma = pltpu.SemaphoreType.DMA
     return pl.pallas_call(
         combine_kernel,
         out_shape=jax.ShapeDtypeStruct((SPAN // NZ, HEAD_SIZE), bf16),
-        in_specs=[pl.BlockSpec(memory_space=pl.ANY), vmem],
+        in_specs=[pl.BlockSpec(memory_space=pl.ANY)] * 2 + [vmem],
         out_specs=vmem,
         scratch_shapes=[
             pltpu.VMEM((QUERY_BLOCK, WIDE), bf16),
@@ -596,26 +695,19 @@
         ],
         compiler_params=pltpu.CompilerParams(collective_id=1, has_side_effects=True),
         name="combine_rows",
-    )(parts, out_weight)
+    )(own_part, parts, out_weight)
 
 
 def local(
     queries, fresh_span_keys, fresh_span_values, context_keys, context_values, selected, out_weight
 ):
-    q_all, span_keys, span_values, pair_k, pair_v = gather(
-        queries, fresh_span_keys, fresh_span_values, context_keys, context_values
+    q_all, span_keys, span_values, pair_k, pair_v, own_part = gather(
+        selected, queries, fresh_span_keys, fresh_span_values, context_keys, context_values
     )
     parts = attend(
-        selected,
-        q_all.reshape(SPAN, HALF),
-        span_keys.reshape(CHIP_TOKENS, HEAD_SIZE),
-        span_values.reshape(CHIP_TOKENS, HEAD_SIZE),
-        context_keys,
-        context_values,
-        pair_k,
-        pair_v,
+        selected, q_all, span_keys, span_values, context_keys, context_values, pair_k, pair_v
     )
-    return combine(parts, out_weight)
+    return combine(own_part, parts, out_weight)
 
 
 def solution(mesh):

time: 79.3 us -> 82.5 us (1.040); the launches traced: 79 us -> 80.8 us
  Pallas kernels: 77.6 us -> 79.5 us
    pallas_call x1, Pallas kernels: 44.1 us -> 51.1 us  [combine(): pl.pallas_call(combine_kernel, out_shape=jax.ShapeDtypeStruct((SPAN // NZ...]
    pallas_call x1, Pallas kernels: 13.3 us -> 7.42 us  [attend(): pl.pallas_call(attend_kernel, out_shape=jax.ShapeDtypeStruct((QUERY_BLOCK...]
where the time goes in v1:
time: 82.5 us; the launch traced here: 80.8 us
  Pallas kernels  79.5 us (96%)
  local copies, waits for them, and re-layouts  1.32 us (2%)
    pallas_call x1, Pallas kernels, combine(): pl.pallas_call(combine_kernel, out_shape=jax.ShapeDtypeStruct((SPAN // NZ...  51.1 us
    pallas_call x1, Pallas kernels, gather(): pl.pallas_call(gather_kernel, out_shape=(jax.ShapeDtypeStruct((SPAN, HALF...  21 us
    pallas_call x1, Pallas kernels, attend(): pl.pallas_call(attend_kernel, out_shape=jax.ShapeDtypeStruct((QUERY_BLOCK...  7.42 us

profile of v1, /device:TPU:6, one launch (start us, length us, event | category | flops | bytes accessed | tf_op | source)
XLA Modules:
  0.0 80.8 jit_solution(13420622418062654192)
XLA Ops:
  0.0 21.0 %gather_spans.1 = (bf16[512,512]{1,0:T(8,128)(2,1)}, bf16[16,128]{1,0:T(8,128)(2,1)}, bf16[16,128]{1,0:T(8,128)(2,1)}, bf16[4096,128]{1,0:T(8,128)(2,1)}, bf16[4...) custom-call(s32[4,12]{1,0:T(4,128)} %sel_ref.3, bf16[8,1024]{1,0:T(8,128)(2,1)} %q_ref.1, bf16[8,128]{1,0:T(8,128)(2,1)} %fk_ref.1, ...), custom_call_target="tpu_custom_call" | custom-call | tf_op jit(solution)/shard_map/gather_spans/pallas_call | solution.py:343
  21.0 7.4 %attend_blocks.1.part_ref = bf16[4,128,640]{2,1,0:T(8,128)(2,1)} custom-call(s32[4,12]{1,0:T(4,128)} %sel_ref.3, bf16[512,512]{1,0:T(8,128)(2,1)} %get-tuple-element.12.q_ref, bf16[16,128]{1,0:T(8,128)(2,1)} %get-tuple-element.13.sk_ref, bf16[16,128]{1,0:T(8,128)(2,1)} %get-tuple-element.14.sv_ref, bf16[4096,128]{1,0:T(8,128)(2,1)} %ck_ref.3, ...), custom_call_target="tpu_custom_call" | custom-call | tf_op jit(solution)/shard_map/attend_blocks/pallas_call | solution.py:444
  28.4 51.1 %combine_rows.1 = bf16[64,128]{1,0:T(8,128)(2,1)} custom-call(bf16[128,640]{1,0:T(8,128)(2,1)} %get-tuple-element.11.own_part_ref, bf16[4,128,640]{2,1,0:T(8,128)(2,1)} %attend_blocks.1.part_ref, bf16[1024,128]{1,0:T(8,128)(2,1)} %w_ref.1), custom_call_target="tpu_custom_call" | custom-call | tf_op jit(solution)/shard_map/combine_rows/pallas_call | solution.py:669
  79.5 1.3 %copy.9 = bf16[64,128]{1,0:T(8,128)(2,1)} copy(bf16[64,128]{1,0:T(8,128)(2,1)} %combine_rows.1) | data formatting | bytes 32768

commit v2 on v1

--- a/solution.py
+++ b/solution.py
@@ -18,6 +18,7 @@
 HALF = CORE_HEADS * HEAD_SIZE
 WIDE = HALF + HEAD_SIZE
 CHIP_TOKENS = 16
+PART_ROWS = QUERY_BLOCK + CHIP_TOKENS
 ROWS = CORE_HEADS * QUERY_BLOCK
 KEY_PIECE = 1024
 PIECES = BLOCK_TOKENS // KEY_PIECE
@@ -134,11 +135,16 @@
     stats = jnp.zeros((QUERY_BLOCK, HEAD_SIZE), jnp.float32)
     for g in range(CORE_HEADS):
         here = slice(g * QUERY_BLOCK, (g + 1) * QUERY_BLOCK)
-        out_ref[:, g * HEAD_SIZE : (g + 1) * HEAD_SIZE] = acc[here].astype(jnp.bfloat16)
+        out_ref[:QUERY_BLOCK, g * HEAD_SIZE : (g + 1) * HEAD_SIZE] = acc[here].astype(jnp.bfloat16)
         stats = jnp.where(stat_lane == g, m_sent[here], stats)
         stats = jnp.where(stat_lane == CORE_HEADS + g, high[here], stats)
         stats = jnp.where(stat_lane == 2 * CORE_HEADS + g, low[here], stats)
-    out_ref[:, HALF:WIDE] = stats.astype(jnp.bfloat16)
+    packed = stats[:CHIP_TOKENS]
+    for n in range(1, NY):
+        packed = packed + pltpu.roll(
+            stats[n * CHIP_TOKENS : (n + 1) * CHIP_TOKENS], n * CHIP_TOKENS, axis=1
+        )
+    out_ref[QUERY_BLOCK:, :HEAD_SIZE] = packed.astype(jnp.bfloat16)
 
 
 def is_wanted(sel_ref, j, block):
@@ -348,7 +354,7 @@
             jax.ShapeDtypeStruct((CHIP_TOKENS, HEAD_SIZE), bf16),
             jax.ShapeDtypeStruct((BLOCK_TOKENS, HEAD_SIZE), bf16),
             jax.ShapeDtypeStruct((BLOCK_TOKENS, HEAD_SIZE), bf16),
-            jax.ShapeDtypeStruct((QUERY_BLOCK, WIDE), bf16),
+            jax.ShapeDtypeStruct((PART_ROWS, HALF), bf16),
         ),
         in_specs=[pl.BlockSpec(memory_space=pltpu.SMEM)] + [anywhere] * 5,
         out_specs=[anywhere] * 6,
@@ -357,7 +363,7 @@
             pltpu.VMEM((QUERY_BLOCK, HALF), bf16),
             pltpu.VMEM((CHIP_TOKENS, HEAD_SIZE), bf16),
             pltpu.VMEM((CHIP_TOKENS, HEAD_SIZE), bf16),
-            pltpu.VMEM((QUERY_BLOCK, WIDE), bf16),
+            pltpu.VMEM((PART_ROWS, HALF), bf16),
             dma((8,)),
             dma((3,)),
             dma((5,)),
@@ -422,14 +428,15 @@
         def _():
             attend_span(chip, j, state, sk_ref, sv_ref)
 
-        @pl.when(n == 1)
-        def _():
-            for copy in copies:
-                copy.wait()
-
         @pl.loop(0, 2)
         def _(b):
             block = jnp.where(b == 0, me, me + 1 - 2 * core)
+            for half in range(2):
+
+                @pl.when(jnp.logical_and(n == 1, b == half))
+                def _():
+                    copies[2 * half].wait()
+                    copies[2 * half + 1].wait()
 
             @pl.when(is_wanted(sel_ref, j, block))
             def _():
@@ -443,7 +450,7 @@
     vmem = pl.BlockSpec(memory_space=pltpu.VMEM)
     return pl.pallas_call(
         attend_kernel,
-        out_shape=jax.ShapeDtypeStruct((QUERY_BLOCKS, QUERY_BLOCK, WIDE), jnp.bfloat16),
+        out_shape=jax.ShapeDtypeStruct((QUERY_BLOCKS, PART_ROWS, HALF), jnp.bfloat16),
         in_specs=[pl.BlockSpec(memory_space=pltpu.SMEM), vmem, vmem, vmem] + [anywhere] * 4,
         out_specs=vmem,
         scratch_shapes=attention_scratch() + [pltpu.SemaphoreType.DMA((4,))],
@@ -451,8 +458,7 @@
     )(selected, q_all, span_keys, span_values, own_k, own_v, pair_k, pair_v)
 
 
-def merge(pieces):
-    stats = [piece[:, HALF:WIDE].astype(jnp.float32) for piece in pieces]
+def merge(pieces, stats):
     joined = []
     for g in range(CORE_HEADS):
         tops = [stat[:, g : g + 1] for stat in stats]
@@ -480,12 +486,15 @@
     out_ref,
     own,
     from_x,
+    from_xs,
     merged,
     from_y,
     rows,
     partial,
     from_z,
     own_sem,
+    s_send,
+    s_recv,
     x_send,
     x_recv,
     y_send,
@@ -543,12 +552,27 @@
             device(0, dy),
         )
 
+    for dx in (2, 1, 3):
+        copy = remote(
+            part_ref.at[lax.rem(x + dx, NX), pl.ds(QUERY_BLOCK, CHIP_TOKENS), pl.ds(0, HEAD_SIZE)],
+            from_xs.at[dx],
+            s_send.at[dx],
+            s_recv.at[dx],
+            device(dx, 0),
+        )
+        copy.start()
+        sends.append(copy)
+
     @pl.loop(0, NY)
     def _(n):
         for dx in (2, 1, 3):
             to_x(dx, turn(n)).start()
 
     mine.wait()
+    for dx in range(1, NX):
+        remote(
+            from_xs.at[dx], from_xs.at[dx], s_send.at[dx], s_recv.at[dx], device(dx, 0)
+        ).wait_recv()
     stat_lane = lax.broadcasted_iota(jnp.int32, (CHIP_TOKENS, HEAD_SIZE), 1)
 
     @pl.loop(0, NY)
@@ -558,7 +582,12 @@
         for dx in range(1, NX):
             spot = from_x.at[dx, here]
             remote(spot, spot, x_send.at[dx, dy], x_recv.at[dx, dy], device(dx, 0)).wait_recv()
-        joined = merge([own[here, :]] + [from_x[dx, here, :] for dx in range(1, NX)])
+        back = lax.rem(NY - at, NY) * CHIP_TOKENS
+        tiles = [own[QUERY_BLOCK:, :HEAD_SIZE]] + [from_xs[dx] for dx in range(1, NX)]
+        joined = merge(
+            [own[here, :]] + [from_x[dx, here, :] for dx in range(1, NX)],
+            [pltpu.roll(tile.astype(f32), back, axis=1) for tile in tiles],
+        )
         stats = jnp.zeros((CHIP_TOKENS, HEAD_SIZE), f32)
         for g, (top, total, acc) in enumerate(joined):
             high = total.astype(jnp.bfloat16).astype(f32)
@@ -576,7 +605,8 @@
         remote(
             from_y.at[dy], from_y.at[dy], y_send.at[dy], y_recv.at[dy], device(0, dy)
         ).wait_recv()
-    joined = merge([merged[y]] + [from_y[dy] for dy in range(1, NY)])
+    pieces = [merged[y]] + [from_y[dy] for dy in range(1, NY)]
+    joined = merge(pieces, [item[:, HALF:].astype(f32) for item in pieces])
     for g, (_, total, acc) in enumerate(joined):
         rows[x, core, y, :, g * HEAD_SIZE : (g + 1) * HEAD_SIZE] = (acc / total).astype(
             jnp.bfloat16
@@ -606,8 +636,7 @@
         copy.start()
         sends.append(copy)
 
-    def project(dx):
-        at = lax.rem(x + NX - dx, NX)
+    def project(at, dx):
         group = rows.at[at, 1 - core]
         remote(group, group, c_send.at[dx], c_recv.at[dx], (other, z)).wait_recv()
         product = jnp.dot(
@@ -628,15 +657,21 @@
                 ).start()
 
     swap(0)
-    project(0)
+    project(x, 0)
     for dx in (1, 3, 2):
         for dy in (0,) + NEAR_FIRST:
             remote(
                 spot(dx, dy), spot(dx, dy), ax_send.at[dx, dy], ax_recv.at[dx, dy], device(dx, 0)
             ).wait_recv()
         swap(dx)
-    for dx in (1, 3, 2):
-        project(dx)
+
+    @pl.loop(0, NX)
+    def _(n):
+        at = lax.rem(z // 2 + 2 + (1 - 2 * lax.rem(n, 2)) * ((n + 1) // 2), NX)
+
+        @pl.when(at != x)
+        def _():
+            project(at, lax.rem(x + NX - at, NX))
 
     total = partial[z].astype(f32)
     for dz in range(1, NZ):
@@ -672,14 +707,17 @@
         in_specs=[pl.BlockSpec(memory_space=pl.ANY)] * 2 + [vmem],
         out_specs=vmem,
         scratch_shapes=[
-            pltpu.VMEM((QUERY_BLOCK, WIDE), bf16),
-            pltpu.VMEM((NX, QUERY_BLOCK, WIDE), bf16),
+            pltpu.VMEM((PART_ROWS, HALF), bf16),
+            pltpu.VMEM((NX, QUERY_BLOCK, HALF), bf16),
+            pltpu.VMEM((NX, CHIP_TOKENS, HEAD_SIZE), bf16),
             pltpu.VMEM((NY, CHIP_TOKENS, WIDE), bf16),
             pltpu.VMEM((NY, CHIP_TOKENS, WIDE), bf16),
             pltpu.VMEM((NX, 2, NY, CHIP_TOKENS, HALF), bf16),
             pltpu.VMEM((NZ, SPAN // NZ, HEAD_SIZE), bf16),
             pltpu.VMEM((NZ, SPAN // NZ, HEAD_SIZE), bf16),
             dma,
+            dma((NX,)),
+            dma((NX,)),
             dma((NX, NY)),
             dma((NX, NY)),
             dma((NY,)),

time: 82.5 us -> 79.6 us (0.965); the launches traced: 80.8 us -> 79.3 us
  Pallas kernels: 79.5 us -> 78 us
    pallas_call x1, Pallas kernels: 51.1 us -> 46.8 us  [combine(): pl.pallas_call(combine_kernel, out_shape=jax.ShapeDtypeStruct((SPAN // NZ...]
    pallas_call x1, Pallas kernels: 7.42 us -> 10.2 us  [attend(): pl.pallas_call(attend_kernel, out_shape=jax.ShapeDtypeStruct((QUERY_BLOCK...]
where the time goes in v2:
time: 79.6 us; the launch traced here: 79.3 us
  Pallas kernels  78 us (98%)
  local copies, waits for them, and re-layouts  1.32 us (2%)
    pallas_call x1, Pallas kernels, combine(): pl.pallas_call(combine_kernel, out_shape=jax.ShapeDtypeStruct((SPAN // NZ...  46.8 us
    pallas_call x1, Pallas kernels, gather(): pl.pallas_call(gather_kernel, out_shape=(jax.ShapeDtypeStruct((SPAN, HALF...  21 us
    pallas_call x1, Pallas kernels, attend(): pl.pallas_call(attend_kernel, out_shape=jax.ShapeDtypeStruct((QUERY_BLOCK...  10.2 us

profile of v2, /device:TPU:6, one launch (start us, length us, event | category | flops | bytes accessed | tf_op | source)
XLA Modules:
  0.0 79.3 jit_solution(12788733858223632742)
XLA Ops:
  0.0 21.0 %gather_spans.1 = (bf16[512,512]{1,0:T(8,128)(2,1)}, bf16[16,128]{1,0:T(8,128)(2,1)}, bf16[16,128]{1,0:T(8,128)(2,1)}, bf16[4096,128]{1,0:T(8,128)(2,1)}, bf16[4...) custom-call(s32[4,12]{1,0:T(4,128)} %sel_ref.3, bf16[8,1024]{1,0:T(8,128)(2,1)} %q_ref.1, bf16[8,128]{1,0:T(8,128)(2,1)} %fk_ref.1, ...), custom_call_target="tpu_custom_call" | custom-call | tf_op jit(solution)/shard_map/gather_spans/pallas_call | solution.py:349
  21.0 10.2 %attend_blocks.1.part_ref = bf16[4,144,512]{2,1,0:T(8,128)(2,1)} custom-call(s32[4,12]{1,0:T(4,128)} %sel_ref.3, bf16[512,512]{1,0:T(8,128)(2,1)} %get-tuple-element.12.q_ref, bf16[16,128]{1,0:T(8,128)(2,1)} %get-tuple-element.13.sk_ref, bf16[16,128]{1,0:T(8,128)(2,1)} %get-tuple-element.14.sv_ref, bf16[4096,128]{1,0:T(8,128)(2,1)} %ck_ref.3, ...), custom_call_target="tpu_custom_call" | custom-call | tf_op jit(solution)/shard_map/attend_blocks/pallas_call | solution.py:451
  31.2 46.8 %combine_rows.1 = bf16[64,128]{1,0:T(8,128)(2,1)} custom-call(bf16[144,512]{1,0:T(8,128)(2,1)} %get-tuple-element.11.own_part_ref, bf16[4,144,512]{2,1,0:T(8,128)(2,1)} %attend_blocks.1.part_ref, bf16[1024,128]{1,0:T(8,128)(2,1)} %w_ref.1), custom_call_target="tpu_custom_call" | custom-call | tf_op jit(solution)/shard_map/combine_rows/pallas_call | solution.py:704
  78.0 1.3 %copy.9 = bf16[64,128]{1,0:T(8,128)(2,1)} copy(bf16[64,128]{1,0:T(8,128)(2,1)} %combine_rows.1) | data formatting | bytes 32768

commit v3 on v2

--- a/solution.py
+++ b/solution.py
@@ -664,14 +664,8 @@
                 spot(dx, dy), spot(dx, dy), ax_send.at[dx, dy], ax_recv.at[dx, dy], device(dx, 0)
             ).wait_recv()
         swap(dx)
-
-    @pl.loop(0, NX)
-    def _(n):
-        at = lax.rem(z // 2 + 2 + (1 - 2 * lax.rem(n, 2)) * ((n + 1) // 2), NX)
-
-        @pl.when(at != x)
-        def _():
-            project(at, lax.rem(x + NX - at, NX))
+    for dx in (1, 3, 2):
+        project(lax.rem(x + NX - dx, NX), dx)
 
     total = partial[z].astype(f32)
     for dz in range(1, NZ):

time: 79.6 us -> 78.7 us (0.989)
    pallas_call x1, Pallas kernels: 10.2 us -> 7.52 us  [attend(): pl.pallas_call(attend_kernel, out_shape=jax.ShapeDtypeStruct((QUERY_BLOCK...]
    pallas_call x1, Pallas kernels: 46.8 us -> 49.3 us  [combine(): pl.pallas_call(combine_kernel, out_shape=jax.ShapeDtypeStruct((SPAN // NZ...]
where the time goes in v3:
time: 78.7 us; the launch traced here: 79.2 us
  Pallas kernels  77.9 us (99%)
  local copies, waits for them, and re-layouts  1.32 us (2%)
    pallas_call x1, Pallas kernels, combine(): pl.pallas_call(combine_kernel, out_shape=jax.ShapeDtypeStruct((SPAN // NZ...  49.3 us
    pallas_call x1, Pallas kernels, gather(): pl.pallas_call(gather_kernel, out_shape=(jax.ShapeDtypeStruct((SPAN, HALF...  21 us
    pallas_call x1, Pallas kernels, attend(): pl.pallas_call(attend_kernel, out_shape=jax.ShapeDtypeStruct((QUERY_BLOCK...  7.52 us

profile of v3, /device:TPU:6, one launch (start us, length us, event | category | flops | bytes accessed | tf_op | source)
XLA Modules:
  0.0 79.2 jit_solution(6948392101525332994)
XLA Ops:
  0.0 21.0 %gather_spans.1 = (bf16[512,512]{1,0:T(8,128)(2,1)}, bf16[16,128]{1,0:T(8,128)(2,1)}, bf16[16,128]{1,0:T(8,128)(2,1)}, bf16[4096,128]{1,0:T(8,128)(2,1)}, bf16[4...) custom-call(s32[4,12]{1,0:T(4,128)} %sel_ref.3, bf16[8,1024]{1,0:T(8,128)(2,1)} %q_ref.1, bf16[8,128]{1,0:T(8,128)(2,1)} %fk_ref.1, ...), custom_call_target="tpu_custom_call" | custom-call | tf_op jit(solution)/shard_map/gather_spans/pallas_call | solution.py:349
  21.0 7.5 %attend_blocks.1.part_ref = bf16[4,144,512]{2,1,0:T(8,128)(2,1)} custom-call(s32[4,12]{1,0:T(4,128)} %sel_ref.3, bf16[512,512]{1,0:T(8,128)(2,1)} %get-tuple-element.12.q_ref, bf16[16,128]{1,0:T(8,128)(2,1)} %get-tuple-element.13.sk_ref, bf16[16,128]{1,0:T(8,128)(2,1)} %get-tuple-element.14.sv_ref, bf16[4096,128]{1,0:T(8,128)(2,1)} %ck_ref.3, ...), custom_call_target="tpu_custom_call" | custom-call | tf_op jit(solution)/shard_map/attend_blocks/pallas_call | solution.py:451
  28.5 49.3 %combine_rows.1 = bf16[64,128]{1,0:T(8,128)(2,1)} custom-call(bf16[144,512]{1,0:T(8,128)(2,1)} %get-tuple-element.11.own_part_ref, bf16[4,144,512]{2,1,0:T(8,128)(2,1)} %attend_blocks.1.part_ref, bf16[1024,128]{1,0:T(8,128)(2,1)} %w_ref.1), custom_call_target="tpu_custom_call" | custom-call | tf_op jit(solution)/shard_map/combine_rows/pallas_call | solution.py:698
  77.9 1.3 %copy.9 = bf16[64,128]{1,0:T(8,128)(2,1)} copy(bf16[64,128]{1,0:T(8,128)(2,1)} %combine_rows.1) | data formatting | bytes 32768
